TPU v7x, 32 devices: a whole 2x2x4 slice. The times are simulated.
32 devices in a mesh: grp: 2 (over y), frm: 4 (over z), row: 4 (over x, core).
Axes of the slice: x: 2, y: 2, z: 4, core: 2. Of those that a mesh axis runs over, the one named last changes fastest.
Arguments:
- hidden_in: bfloat16 [512, 16, 2240], P('row', ('grp', 'frm')), parts along dimension 1, may hold values from -6 to 6
- norm_gain: float32 [2240], replicated, may hold values from 0.1 to 1.9
- query_key_value_weight: bfloat16 [2240, 3, 2240], P(None, None, 'row'), may hold values from -0.125 to 0.125
- head_gain: float32 [2240], P('row'), may hold values from 0.1 to 1.9
- output_matrix: bfloat16 [2240, 2240], P('row'), may hold values from -0.125 to 0.125
- block_end: int32 [16], P(('grp', 'frm')), parts along dimension 0, may hold values from 0 to 7, as said below
Outputs:
- mixed_out: bfloat16 [512, 16, 2240], P('row', ('grp', 'frm')), parts along dimension 1
There are 2 independent parts, one for each index of `grp`. A program takes and returns all parts, laid end to end along the dimension named above; an argument that names none is the same for every part. Nothing has to cross between parts.
Inputs may be any that keep to these rules, and one draw needn't show every extreme that they name: `block_end`: entries never fall from one frame to the next; each entry is at least its frame's index, and frames with equal entries form a block of consecutive frames; a block never holds frames of two different runs of 2 frames (f // 2 differs), and the last frame of every such run ends a block.
All inputs are finite; a program needn't handle non-finite values.
Results may differ from a plain program's by a relative error of at most 0.015.
Values may be sent and summed in bfloat16 or wider, within the bound.
No kernel may reach another device: no remote copies, remote signals or barrier semaphores. Data moves between devices by JAX's collectives and lax.ppermute only.
A program may use at most 64 MiB of HBM per device.

v0:
```python
import jax
import jax.numpy as jnp
from jax import lax
from jax.sharding import PartitionSpec as P

HD = 112
epsilon = 1e-06


def per_device(hidden_in, norm_gain, query_key_value_weight, head_gain, output_matrix, block_end):
    slab_rows, own_frames, model_width = hidden_in.shape
    local_heads = head_gain.shape[0] // HD
    group_width = local_heads * HD
    as_float = hidden_in.astype(jnp.float32)
    mean_square = jnp.mean(as_float * as_float, axis=-1, keepdims=True)
    normed = (as_float * lax.rsqrt(mean_square + epsilon) * norm_gain).astype(jnp.bfloat16)
    weights = query_key_value_weight.reshape(model_width, 3 * group_width)
    rows_per_block = lax.all_gather(normed, "row", axis=0, tiled=True)
    flat = rows_per_block.reshape(-1, model_width)
    result = jnp.dot(flat, weights, preferred_element_type=jnp.float32).astype(jnp.bfloat16)
    projected = result.reshape(rows_per_block.shape[0], own_frames, 3 * group_width)
    projected = projected.reshape(-1, own_frames, 3, local_heads, HD)
    queries = jax.nn.relu(projected[:, :, 0])
    key_relu = jax.nn.relu(projected[:, :, 1])
    values = projected[:, :, 2]
    per_frame_state = jnp.einsum(
        "pfhi,pfhj->fhij", key_relu, values, preferred_element_type=jnp.float32
    )
    per_device_sum = jnp.sum(per_frame_state, axis=0)
    earlier_mask = (block_end[None, :] <= block_end[:, None]).astype(jnp.float32)
    inside = jnp.einsum(
        "fg,ghij->fhij", earlier_mask, per_frame_state, precision=lax.Precision.HIGHEST
    )
    my_index = lax.axis_index("frm")
    rows_per_block = lax.all_gather(
        per_device_sum[None].astype(jnp.bfloat16), "frm", axis=0, tiled=True
    ).astype(jnp.float32)
    owners = jnp.arange(rows_per_block.shape[0], dtype=jnp.int32)
    include = (owners < my_index).astype(jnp.float32)
    prior_frames_sum = jnp.zeros_like(per_device_sum) + jnp.einsum(
        "n,nhij->hij", include, rows_per_block, precision=lax.Precision.HIGHEST
    )
    block_state = (inside + prior_frames_sum[None]).astype(jnp.bfloat16)
    attended = jnp.einsum(
        "pfhi,fhij->pfhj", queries, block_state, preferred_element_type=jnp.float32
    )
    head_square = jnp.mean(attended * attended, axis=-1, keepdims=True)
    head_out = (
        attended * lax.rsqrt(head_square + epsilon) * head_gain.reshape(local_heads, HD)
    ).astype(jnp.bfloat16)
    merged_heads = head_out.reshape(head_out.shape[0], own_frames, group_width)
    own_tokens = lax.all_to_all(merged_heads, "row", split_axis=0, concat_axis=2, tiled=True)
    rows_per_block = lax.all_gather(output_matrix, "row", axis=0, tiled=True)
    shards = rows_per_block.shape[0] // group_width
    split_cols = own_tokens.reshape(slab_rows, own_frames, shards, group_width)
    split_rows = rows_per_block.reshape(shards, group_width, model_width)
    products = jnp.einsum(
        "pfkc,kcd->kpfd", split_cols, split_rows, preferred_element_type=jnp.float32
    )
    rounded = lax.optimization_barrier(products.astype(jnp.bfloat16)).astype(jnp.float32)
    summed = jnp.sum(rounded, axis=0)
    return summed.astype(jnp.bfloat16)


def solution(mesh):
    placed = (
        P("row", ("grp", "frm"), None),
        P(),
        P(None, None, "row"),
        P("row"),
        P("row", None),
        P(("grp", "frm")),
    )
    return jax.shard_map(
        per_device,
        mesh=mesh,
        in_specs=placed,
        out_specs=P("row", ("grp", "frm"), None),
        check_vma=False,
    )
```

profile of v0, /device:TPU:0, one launch (start us, length us, event | category | flops | bytes accessed | tf_op | source)
XLA Modules:
  0.0 184.6 jit_solution(13249381109375235139)
XLA Ops:
  6.5 1.6 fusion
  8.1 2.6 %fusion.2 = bf16[128,2,2240]{0,2,1:T(8,128)(2,1)} fusion(bf16[128,2,2240]{0,2,1:T(8,128)(2,1)} %param.6, f32[2240]{0:T(1024)} %param.7, f32[128,2]{0,1:T(2,128)S(1)} %add_rsqrt_fusion.1), kind=kLoop, calls=%fused_computation.6 | loop fusion | flops 2293760 | bytes 2303744 | tf_op jit(solution)/shard_map/convert_element_type | solution.py:16
  10.8 0.7 all-gather.6.cloned.1.call-update
  11.6 39.3 %all-gather.4.cloned.1.call-done = bf16[512,2,2240]{0,2,1:T(8,128)(2,1)} async-done(((bf16[128,2,2240]{0,2,1:T(8,128)(2,1)}), bf16[512,2,2240]{0,2,1:T(8,128)(2,1)}) %all-gather.4.cloned.1.call-update) | async-done | bytes 4587536 | tf_op jit(solution)/shard_map/all_gather | solution.py:18
  50.9 12.8 %copy.16 = bf16[512,2,2240]{2,1,0:T(2,128)(2,1)} copy(bf16[512,2,2240]{0,2,1:T(8,128)(2,1)} %all-gather.4.cloned.1.call-done) | data formatting | bytes 9175040 | tf_op jit(solution)/shard_map/all_gather | solution.py:18
  63.8 10.8 %reshape.48 = bf16[1024,2240]{1,0:T(8,128)(2,1)} reshape(bf16[512,2,2240]{2,1,0:T(2,128)(2,1)} %copy.16) | data formatting | bytes 9175040 | tf_op jit(solution)/shard_map/reshape | solution.py:19
  74.5 11.9 %convolution_convert_fusion.1 = bf16[1024,1680]{0,1:T(8,128)(2,1)S(1)} fusion(bf16[1024,2240]{1,0:T(8,128)(2,1)} %reshape.48, bf16[2240,1680]{0,1:T(8,128)(2,1)} %bitcast.55), kind=kOutput, calls=%fused_computation.1 | convolution fusion | flops 7708753920 | bytes 15554560 | tf_op jit(solution)/shard_map/dot_general | solution.py:20
  86.5 3.8 %copy.17 = bf16[1024,1680]{1,0:T(8,128)(2,1)} copy(bf16[1024,1680]{0,1:T(8,128)(2,1)S(1)} %convolution_convert_fusion.1) | data formatting | bytes 6881280 | tf_op jit(solution)/shard_map/convert_element_type | solution.py:20
  90.2 11.4 %reshape_reshape.3 = bf16[512,2,3,5,112]{4,3,2,1,0:T(8,128)(2,1)} reshape(bf16[1024,1680]{1,0:T(8,128)(2,1)} %copy.17) | data formatting | bytes 6881280 | tf_op jit(solution)/shard_map/reshape;reshape | solution.py:22
  101.7 5.9 %fusion.29 = (bf16[512,2,1,5,112]{4,3,2,1,0:T(8,128)(2,1)}, bf16[512,2,1,5,112]{4,3,2,1,0:T(8,128)(2,1)}, bf16[512,2,1,5,112]{4,3,2,1,0:T(8,128)(2,1)S(1)}) fusion(bf16[512,2,3,5,112]{4,3,2,1,0:T(8,128)(2,1)} %reshape_reshape.3), kind=kLoop, calls=%fused_computation.39 | loop fusion | bytes 6881280 | tf_op jit(solution)/shard_map/slice | solution.py:24
  107.6 4.1 %copy.33 = bf16[512,2,1,5,112]{0,4,3,1,2:T(8,128)(2,1)} copy(bf16[512,2,1,5,112]{4,3,2,1,0:T(8,128)(2,1)} %get-tuple-element.5) | data formatting | bytes 2293760
  111.6 4.1 %copy.34 = bf16[512,2,1,5,112]{0,4,3,1,2:T(8,128)(2,1)} copy(bf16[512,2,1,5,112]{4,3,2,1,0:T(8,128)(2,1)} %get-tuple-element.6) | data formatting | bytes 2293760
  115.7 1.4 copy.35
  117.1 2.1 %fusion.30 = (bf16[5,112,112]{2,1,0:T(8,128)(2,1)S(1)}, f32[2,5,112,112]{3,2,1,0:T(8,128)S(1)}) fusion(bf16[512,2,1,5,112]{0,4,3,1,2:T(8,128)(2,1)} %copy.34, bf16[512,2,1,5,112]{0,4,3,1,2:T(8,128)(2,1)} %copy.33), kind=kOutput, calls=%fused_computation.40 | convolution fusion | flops 129086720 | bytes 2920960 | tf_op jit(solution)/shard_map/pfhi,pfhj->fhij/dot_general | solution.py:26
  119.2 17.1 %all-gather = bf16[20,112,112]{2,1,0:T(8,128)(2,1)S(1)} all-gather(bf16[5,112,112]{2,1,0:T(8,128)(2,1)S(1)} %get-tuple-element.8), channel_id=2, replica_groups=mesh['grp'=2,'frm'=4,'row'=4] {'frm'}, dimensions={0}, use_global_device_ids=true | all-gather | bytes 627200 | tf_op jit(solution)/shard_map/all_gather | solution.py:35
  136.3 0.4 fusion.18
  136.7 1.5 fusion.6
  138.2 0.5 fusion.3
  138.8 0.3 fusion.5
  139.1 1.9 %copy.23 = bf16[512,2,560]{2,1,0:T(2,128)(2,1)S(1)} copy(bf16[512,2,560]{0,2,1:T(8,128)(2,1)S(1)} %bitcast.52) | data formatting | bytes 2293760 | tf_op jit(solution)/shard_map/reshape | solution.py:51
  141.0 19.7 %all_to_all.15 = bf16[512,2,560]{2,1,0:T(2,128)(2,1)S(1)} all-to-all(bf16[512,2,560]{2,1,0:T(2,128)(2,1)S(1)} %copy.23), channel_id=1, replica_groups=mesh['grp'=2,'frm'=4,'row'=4] {'row'}, dimensions={0} | all-to-all | bytes 2293760 | tf_op jit(solution)/shard_map/all_to_all | solution.py:52
  160.7 2.0 %copy.25 = bf16[4,128,2,560]{1,3,2,0:T(8,128)(2,1)S(1)} copy(bf16[4,128,2,560]{3,2,1,0:T(2,128)(2,1)S(1)} %bitcast.51) | data formatting | bytes 2293760 | tf_op jit(solution)/shard_map/all_to_all | solution.py:52
  162.7 10.8 %convolution_convert_fusion = bf16[4,128,2,2240]{1,3,2,0:T(8,128)(2,1)} fusion(bf16[4,560,2240,1]{2,1,3,0:T(8,128)(2,1)} %bitcast.54, bf16[4,128,2,560]{1,3,2,0:T(8,128)(2,1)S(1)} %copy.25), kind=kOutput, calls=%fused_computation | convolution fusion | flops 2571304960 | bytes 15769600 | tf_op jit(solution)/shard_map/pfkc,kcd->kpfd/dot_general | solution.py:57
  173.5 4.3 %reduce_sum.42 = bf16[128,2,2240]{0,2,1:T(8,128)(2,1)} reduce(bf16[4,128,2,2240]{1,3,2,0:T(8,128)(2,1)} %convolution_convert_fusion, bf16[]{:T(256)} %constant.17.clone.1), dimensions={0}, to_apply=%region_3.4 | reduce | flops 1720320 | bytes 5734402 | tf_op jit(solution)/shard_map/reduce_sum | solution.py:61
  (11 shorter events, 0.2 us)
Async XLA Ops:
  6.5 44.4 %all-gather.4.cloned.1.call-start = ((), (), s32[]{:S(2)}) async-start(), calls=%async_computation.1 | async-start | bytes 5734400 | tf_op jit(solution)/shard_map/all_gather | solution.py:18
  10.8 0.8 copy-start
  10.8 151.9 %all-gather.6.cloned.1.call-start = ((), (), s32[]{:S(2)}) async-start(), calls=%async_computation.2 | async-start | bytes 12902400 | tf_op jit(solution)/shard_map/all_gather | solution.py:53
  117.1 19.6 %copy-start.1 = (s32[2]{0:T(128)S(1)}, s32[2]{0:T(128)}, u32[]{:S(2)}) copy-start(s32[2]{0:T(128)} %param.11) | copy-start | bytes 28
Sparse Core Ops, SparseCore 0:
  10.9 39.9 all-gather.3
  52.5 69.2 all-gather.5
where the time goes:
time: 186 us; the launch traced here: 185 us
  local copies, waits for them, and re-layouts  58.2 us (31%)
  waiting for transfers between devices  40.1 us (22%)
  blocking collectives  36.8 us (20%)
  matrix products  27.2 us (15%)
  between operations  13.5 us (7%)
  other arithmetic  8.82 us (5%)
    all_gather x1, waiting for transfers between devices, per_device(): rows_per_block = lax.all_gather(normed, 'row', axis=0, tiled=True)  39.3 us
    all_to_all x1, blocking collectives, per_device(): lax.all_to_all(merged_heads, 'row', split_axis=0, concat_axis=2, tiled=True)  19.7 us
    all_gather x1, blocking collectives, per_device(): lax.all_gather(per_device_sum[None].astype(jnp.bfloat16), 'frm', axis=0,...  17.1 us
    all_gather x1, local copies, waits for them, and re-layouts, per_device(): rows_per_block = lax.all_gather(normed, 'row', axis=0, tiled=True)  12.8 us
    dot_general x1, matrix products, per_device(): jnp.dot(flat, weights, preferred_element_type=jnp.float32)  11.9 us
    another operation x1, local copies, waits for them, and re-layouts, per_device(): projected = projected.reshape(-1, own_frames, 3, local_heads, HD)  11.4 us
    dot_general x1, matrix products, per_device(): jnp.einsum('pfkc,kcd->kpfd', split_cols, split_rows, preferred_element_ty...  10.8 us
    reshape x1, local copies, waits for them, and re-layouts, per_device(): flat = rows_per_block.reshape(-1, model_width)  10.8 us
  transfers between devices with their start and end apart: 2, of which 1 were waited for; matrix products, arithmetic and copies ran while one was open for 41% of the time, Pallas kernels for 0%

commit v1 on v0

--- a/solution.py
+++ b/solution.py
@@ -49,7 +49,12 @@
         attended * lax.rsqrt(head_square + epsilon) * head_gain.reshape(local_heads, HD)
     ).astype(jnp.bfloat16)
     merged_heads = head_out.reshape(head_out.shape[0], own_frames, group_width)
-    own_tokens = lax.all_to_all(merged_heads, "row", split_axis=0, concat_axis=2, tiled=True)
+    own_tokens = jnp.concatenate(
+        lax.all_to_all(
+            jnp.stack(jnp.split(merged_heads, lax.axis_size("row"), axis=0)), "row", 0, 0
+        ),
+        axis=2,
+    )
     rows_per_block = lax.all_gather(output_matrix, "row", axis=0, tiled=True)
     shards = rows_per_block.shape[0] // group_width
     split_cols = own_tokens.reshape(slab_rows, own_frames, shards, group_width)

time: 186 us -> 180 us (0.968)
  local copies, waits for them, and re-layouts: 58.2 us -> 54.5 us
  blocking collectives: 36.8 us -> 34.8 us
    all_to_all x1 -> x0, local copies, waits for them, and re-layouts: 1.97 us -> none  [per_device(): lax.all_to_all(merged_heads, 'row', split_axis=0, concat_axis=2, tiled=True)]
    reshape x1 -> x0, local copies, waits for them, and re-layouts: 1.94 us -> none  [per_device(): merged_heads = head_out.reshape(head_out.shape[0], own_frames, group_width)]
  transfers between devices with their start and end apart: 2 -> 2, of which waited for: 1 -> 1; matrix products, arithmetic and copies ran while one was open for 41% -> 40% of each run, Pallas kernels for 0% -> 0%
where the time goes in v1:
time: 180 us; the launch traced here: 179 us
  local copies, waits for them, and re-layouts  54.5 us (30%)
  waiting for transfers between devices  40 us (22%)
  blocking collectives  34.8 us (19%)
  matrix products  27.2 us (15%)
  between operations  13.5 us (8%)
  other arithmetic  8.96 us (5%)
    all_gather x1, waiting for transfers between devices, per_device(): rows_per_block = lax.all_gather(normed, 'row', axis=0, tiled=True)  39.3 us
    all_to_all x1, blocking collectives, per_device(): lax.all_to_all(jnp.stack(jnp.split(merged_heads, lax.axis_size('row'), ax...  17.9 us
    all_gather x1, blocking collectives, per_device(): lax.all_gather(per_device_sum[None].astype(jnp.bfloat16), 'frm', axis=0,...  16.9 us
    all_gather x1, local copies, waits for them, and re-layouts, per_device(): rows_per_block = lax.all_gather(normed, 'row', axis=0, tiled=True)  12.8 us
    dot_general x1, matrix products, per_device(): jnp.dot(flat, weights, preferred_element_type=jnp.float32)  11.9 us
    another operation x1, local copies, waits for them, and re-layouts, per_device(): projected = projected.reshape(-1, own_frames, 3, local_heads, HD)  11.4 us
    dot_general x1, matrix products, per_device(): jnp.einsum('pfkc,kcd->kpfd', split_cols, split_rows, preferred_element_ty...  10.8 us
    reshape x1, local copies, waits for them, and re-layouts, per_device(): flat = rows_per_block.reshape(-1, model_width)  10.8 us
  transfers between devices with their start and end apart: 2, of which 1 were waited for; matrix products, arithmetic and copies ran while one was open for 40% of the time, Pallas kernels for 0%

profile of v1, /device:TPU:0, one launch (start us, length us, event | category | flops | bytes accessed | tf_op | source)
XLA Modules:
  0.0 179.1 jit_solution(15093926075854131767)
XLA Ops:
  6.5 1.6 fusion
  8.1 2.6 %fusion.2 = bf16[128,2,2240]{0,2,1:T(8,128)(2,1)} fusion(bf16[128,2,2240]{0,2,1:T(8,128)(2,1)} %param.6, f32[2240]{0:T(1024)} %param.7, f32[128,2]{0,1:T(2,128)S(1)} %add_rsqrt_fusion.1), kind=kLoop, calls=%fused_computation.6 | loop fusion | flops 2293760 | bytes 2303744 | tf_op jit(solution)/shard_map/convert_element_type | solution.py:16
  10.8 0.7 all-gather.6.cloned.1.call-update
  11.6 39.3 %all-gather.4.cloned.1.call-done = bf16[512,2,2240]{0,2,1:T(8,128)(2,1)} async-done(((bf16[128,2,2240]{0,2,1:T(8,128)(2,1)}), bf16[512,2,2240]{0,2,1:T(8,128)(2,1)}) %all-gather.4.cloned.1.call-update) | async-done | bytes 4587536 | tf_op jit(solution)/shard_map/all_gather | solution.py:18
  50.9 12.8 %copy.15 = bf16[512,2,2240]{2,1,0:T(2,128)(2,1)} copy(bf16[512,2,2240]{0,2,1:T(8,128)(2,1)} %all-gather.4.cloned.1.call-done) | data formatting | bytes 9175040 | tf_op jit(solution)/shard_map/all_gather | solution.py:18
  63.8 10.8 %reshape.55 = bf16[1024,2240]{1,0:T(8,128)(2,1)} reshape(bf16[512,2,2240]{2,1,0:T(2,128)(2,1)} %copy.15) | data formatting | bytes 9175040 | tf_op jit(solution)/shard_map/reshape | solution.py:19
  74.5 11.9 %convolution_convert_fusion.1 = bf16[1024,1680]{0,1:T(8,128)(2,1)S(1)} fusion(bf16[1024,2240]{1,0:T(8,128)(2,1)} %reshape.55, bf16[2240,1680]{0,1:T(8,128)(2,1)} %bitcast.59), kind=kOutput, calls=%fused_computation.1 | convolution fusion | flops 7708753920 | bytes 15554560 | tf_op jit(solution)/shard_map/dot_general | solution.py:20
  86.5 3.7 %copy.16 = bf16[1024,1680]{1,0:T(8,128)(2,1)} copy(bf16[1024,1680]{0,1:T(8,128)(2,1)S(1)} %convolution_convert_fusion.1) | data formatting | bytes 6881280 | tf_op jit(solution)/shard_map/convert_element_type | solution.py:20
  90.2 11.4 %reshape_reshape.3 = bf16[512,2,3,5,112]{4,3,2,1,0:T(8,128)(2,1)} reshape(bf16[1024,1680]{1,0:T(8,128)(2,1)} %copy.16) | data formatting | bytes 6881280 | tf_op jit(solution)/shard_map/reshape;reshape | solution.py:22
  101.6 5.9 %fusion.29 = (bf16[512,2,1,5,112]{4,3,2,1,0:T(8,128)(2,1)}, bf16[512,2,1,5,112]{4,3,2,1,0:T(8,128)(2,1)}, bf16[512,2,1,5,112]{4,3,2,1,0:T(8,128)(2,1)S(1)}) fusion(bf16[512,2,3,5,112]{4,3,2,1,0:T(8,128)(2,1)} %reshape_reshape.3), kind=kLoop, calls=%fused_computation.40 | loop fusion | bytes 6881280 | tf_op jit(solution)/shard_map/slice | solution.py:24
  107.6 4.1 %copy.27 = bf16[512,2,1,5,112]{0,4,3,1,2:T(8,128)(2,1)} copy(bf16[512,2,1,5,112]{4,3,2,1,0:T(8,128)(2,1)} %get-tuple-element.5) | data formatting | bytes 2293760
  111.6 4.1 %copy.28 = bf16[512,2,1,5,112]{0,4,3,1,2:T(8,128)(2,1)} copy(bf16[512,2,1,5,112]{4,3,2,1,0:T(8,128)(2,1)} %get-tuple-element.6) | data formatting | bytes 2293760
  115.7 1.4 copy.29
  117.1 2.1 %fusion.31 = (bf16[5,112,112]{2,1,0:T(8,128)(2,1)S(1)}, f32[2,5,112,112]{3,2,1,0:T(8,128)S(1)}) fusion(bf16[512,2,1,5,112]{0,4,3,1,2:T(8,128)(2,1)} %copy.28, bf16[512,2,1,5,112]{0,4,3,1,2:T(8,128)(2,1)} %copy.27), kind=kOutput, calls=%fused_computation.42 | convolution fusion | flops 129086720 | bytes 2920960 | tf_op jit(solution)/shard_map/pfhi,pfhj->fhij/dot_general | solution.py:26
  119.2 16.9 %all-gather = bf16[20,112,112]{2,1,0:T(8,128)(2,1)S(1)} all-gather(bf16[5,112,112]{2,1,0:T(8,128)(2,1)S(1)} %get-tuple-element.12), channel_id=2, replica_groups=mesh['grp'=2,'frm'=4,'row'=4] {'frm'}, dimensions={0}, use_global_device_ids=true | all-gather | bytes 627200 | tf_op jit(solution)/shard_map/all_gather | solution.py:35
  136.1 0.4 fusion.18
  136.6 1.5 fusion.6
  138.0 0.5 fusion.3
  138.6 0.3 fusion.5
  138.9 0.2 fusion.30
  139.1 0.1 pad_maximum_fusion
  139.2 17.9 %all_to_all.5 = bf16[4,128,2,560]{1,3,2,0:T(8,128)(2,1)S(1)} all-to-all(bf16[4,128,2,560]{1,3,2,0:T(8,128)(2,1)S(1)} %pad_maximum_fusion), channel_id=1, replica_groups=mesh['grp'=2,'frm'=4,'row'=4] {'row'}, dimensions={0} | all-to-all | bytes 2293760 | tf_op jit(solution)/shard_map/all_to_all | solution.py:53
  157.1 10.8 %convolution_convert_fusion = bf16[4,128,2,2240]{1,3,2,0:T(8,128)(2,1)} fusion(bf16[4,560,2240,1]{2,1,3,0:T(8,128)(2,1)} %bitcast.58, bf16[4,128,2,560]{1,3,2,0:T(8,128)(2,1)S(1)} %all_to_all.5), kind=kOutput, calls=%fused_computation | convolution fusion | flops 2571304960 | bytes 15769600 | tf_op jit(solution)/shard_map/pfkc,kcd->kpfd/dot_general | solution.py:62
  167.9 4.3 %reduce_sum.42 = bf16[128,2,2240]{0,2,1:T(8,128)(2,1)} reduce(bf16[4,128,2,2240]{1,3,2,0:T(8,128)(2,1)} %convolution_convert_fusion, bf16[]{:T(256)} %constant.17.clone.1), dimensions={0}, to_apply=%region_3.4 | reduce | flops 1720320 | bytes 5734402 | tf_op jit(solution)/shard_map/reduce_sum | solution.py:66
  (11 shorter events, 0.2 us)
Async XLA Ops:
  6.5 44.4 %all-gather.4.cloned.1.call-start = ((), (), s32[]{:S(2)}) async-start(), calls=%async_computation.1 | async-start | bytes 5734400 | tf_op jit(solution)/shard_map/all_gather | solution.py:18
  10.8 0.8 copy-start
  10.8 146.4 %all-gather.6.cloned.1.call-start = ((), (), s32[]{:S(2)}) async-start(), calls=%async_computation.2 | async-start | bytes 12902400 | tf_op jit(solution)/shard_map/all_gather | solution.py:58
  117.1 19.5 %copy-start.1 = (s32[2]{0:T(128)S(1)}, s32[2]{0:T(128)}, u32[]{:S(2)}) copy-start(s32[2]{0:T(128)} %param.11) | copy-start | bytes 28
Sparse Core Ops, SparseCore 0:
  10.9 39.9 all-gather.3
  52.5 69.2 all-gather.5
